TPU v7x, 256 devices: a whole 4x4x8 slice. The times are simulated.
256 devices in a mesh: segment: 2 (over core), seq: 128 (over x, y, z).
Axes of the slice: x: 4, y: 4, z: 8, core: 2. Of those that a mesh axis runs over, the one named last changes fastest.
Arguments:
- activations: bfloat16 [2, 32768, 768], P('segment', 'seq'), may hold values from -6 to 6
- short_filters: bfloat16 [2, 128, 768], replicated, may hold values from -0.5 to 0.5
- long_filters: float32 [2, 32768, 768], P('segment', 'seq'), may hold values from -4 to 4
- skip_gain: float32 [2, 768], replicated, may hold values from -1 to 1
Outputs:
- sections: bfloat16 [2, 32768, 768], P('segment', 'seq')
All inputs are finite; a program needn't handle non-finite values.
Results may differ from a plain program's by a relative error of at most 0.012.
Values may be sent and summed in bfloat16 or wider, within the bound.
A program may use at most 64 MiB of HBM per device.

v0:
```python
import functools
import math

import jax
import jax.numpy as jnp
import numpy as np
from jax import lax
from jax.experimental import pallas as pl
from jax.experimental.pallas import tpu as pltpu
from jax.sharding import PartitionSpec as P

KP = 144


def tables(rows, cols, width):
    half = rows // 2
    k1 = np.arange(KP)
    live = (k1 <= half).astype(np.float64)
    a = np.arange(width)
    ph = 2.0 * np.pi * ((k1[:, None] * a[None, :]) % rows) / rows
    row_fwd = np.concatenate([np.cos(ph) * live[:, None], -np.sin(ph) * live[:, None]], 0)
    weight = live * np.where((k1 == 0) | (k1 == half), 1.0, 2.0)
    row_back = np.concatenate([(np.cos(ph) * weight[:, None]).T, (-np.sin(ph) * weight[:, None]).T], 1)
    b = np.arange(cols)
    pc = 2.0 * np.pi * ((b[:, None] * b[None, :]) % cols) / cols
    c, s = np.cos(pc), np.sin(pc)
    col_fwd = np.block([[c, -s], [s, c]])
    col_back = np.block([[c, s], [-s, c]])
    tw = 2.0 * np.pi * ((k1[:, None] * b[None, :]) % (rows * cols)) / (rows * cols)
    bf = lambda x: jnp.asarray(x, jnp.bfloat16)
    return (
        bf(row_fwd), bf(row_back), bf(col_fwd), bf(col_back),
        jnp.asarray(np.stack([np.cos(tw), np.sin(tw)]), jnp.float32),
    )


def dot(a, b):
    return jnp.dot(a, b, preferred_element_type=jnp.float32)


def filter_kernel(scale, x_ref, f_ref, taps_ref, gain_ref, rf_ref, rb_ref, cf_ref, cb_ref, tw_ref,
                  out_ref, pad_ref):
    channels = x_ref.shape[1]
    rows, cols = x_ref.shape[2], x_ref.shape[3]
    b_in = lax.broadcasted_iota(jnp.int32, (cols, cols), 0)
    b_out = lax.broadcasted_iota(jnp.int32, (cols, cols), 1)

    def spectrum(grid):
        first = dot(rf_ref[...], grid)
        re, im = first[:KP], first[KP:]
        cosine, sine = tw_ref[0], tw_ref[1]
        turned = jnp.concatenate(
            [re * cosine + im * sine, im * cosine - re * sine], 1
        ).astype(jnp.bfloat16)
        return dot(turned, cf_ref[...])

    def inverse(product):
        back = dot(product, cb_ref[...])
        re, im = back[:, :cols], back[:, cols:]
        cosine, sine = tw_ref[0], tw_ref[1]
        turned = jnp.concatenate(
            [re * cosine - im * sine, re * sine + im * cosine], 0
        ).astype(jnp.bfloat16)
        return dot(rb_ref[...], turned) * scale

    def short(grid, taps):
        circ = pltpu.roll(
            jnp.broadcast_to(taps, (cols, cols)), 0, 1, stride=1, stride_axis=0
        )
        now = jnp.where(b_out >= b_in, circ, 0.0).astype(jnp.bfloat16)
        before = jnp.where(b_out < b_in, circ, 0.0).astype(jnp.bfloat16)
        pad_ref[8:, :] = grid.astype(jnp.float32)
        earlier = pad_ref[7:7 + rows, :].astype(jnp.bfloat16)
        return (dot(grid, now) + dot(earlier, before)).astype(jnp.bfloat16)

    pad_ref[...] = jnp.zeros_like(pad_ref)
    for c in range(channels):
        previous = None
        for s in range(2):
            grid = x_ref[s, c]
            if s:
                grid = (previous.astype(jnp.float32) * grid.astype(jnp.float32)).astype(jnp.bfloat16)
            z = short(grid, taps_ref[s * channels + c][None, :])
            signal = spectrum(z)
            kernel_spec = spectrum(f_ref[s, c])
            ar, ai = signal[:, :cols], signal[:, cols:]
            hr, hi = kernel_spec[:, :cols], kernel_spec[:, cols:]
            product = jnp.concatenate([ar * hr - ai * hi, ar * hi + ai * hr], 1).astype(jnp.bfloat16)
            long = inverse(product).astype(jnp.bfloat16).astype(jnp.float32)
            previous = (long + gain_ref[s, c] * z.astype(jnp.float32)).astype(jnp.bfloat16)
            out_ref[s, c] = previous


def body(activations, short_filters, long_filters, skip_gain):
    tokens, width = activations.shape[1:]
    segs, seqs = lax.axis_size("segment"), lax.axis_size("seq")
    parts = segs * seqs
    mine = width // parts
    cols, rows = tokens, 2 * seqs
    both = ("seq", "segment")
    first = (lax.axis_index("seq") * segs + lax.axis_index("segment")) * mine
    taps = lax.dynamic_slice_in_dim(short_filters, first, mine, 2)
    taps = jnp.swapaxes(taps, 1, 2).reshape(2 * mine, -1).astype(jnp.float32)
    taps = jnp.pad(taps, ((0, 0), (0, cols - taps.shape[1])))
    gains = lax.dynamic_slice_in_dim(skip_gain, first, mine, 1)

    def outward(block):
        turned = block.T.reshape(parts, mine, tokens)
        got = lax.all_to_all(turned, both, 0, 0, tiled=True)
        return got.reshape(seqs, segs, mine, tokens).transpose(1, 2, 0, 3)

    x = outward(activations[0])
    f = outward(long_filters[0].astype(jnp.bfloat16))
    scale = 1.0 / (rows * cols * math.sqrt(rows * cols // 2))
    vm = pl.BlockSpec(memory_space=pltpu.VMEM)
    sm = pl.BlockSpec(memory_space=pltpu.SMEM)
    out = pl.pallas_call(
        functools.partial(filter_kernel, scale),
        out_shape=jax.ShapeDtypeStruct((2, mine, seqs, tokens), jnp.bfloat16),
        in_specs=[vm, vm, vm, sm, vm, vm, vm, vm, vm],
        out_specs=vm,
        scratch_shapes=[pltpu.VMEM((seqs + 8, cols), jnp.float32)],
        compiler_params=pltpu.CompilerParams(vmem_limit_bytes=56 * 1024 * 1024),
    )(x, f, taps, gains, *tables(rows, cols, seqs))
    home = out.transpose(2, 0, 1, 3).reshape(parts, mine, tokens)
    back = lax.all_to_all(home, both, 0, 0, tiled=True)
    return back.reshape(width, tokens).T[None]


def solution(mesh):
    return jax.shard_map(
        body,
        mesh=mesh,
        in_specs=(P("segment", "seq", None), P(), P("segment", "seq", None), P()),
        out_specs=P("segment", "seq", None),
        check_vma=False,
    )
```

profile of v0, /device:TPU:1, one launch (start us, length us, event | category | flops | bytes accessed | tf_op | source)
XLA Modules:
  0.0 105.4 jit_solution(17984082890872431712)
XLA Ops:
  0.0 0.0 copy-start
  0.0 1.2 %copy.21 = bf16[768,256]{1,0:T(8,128)(2,1)S(1)} copy(bf16[768,256]{0,1:T(8,128)(2,1)} %bitcast.29) | data formatting | bytes 786432 | tf_op jit(solution)/shard_map/transpose | solution.py:108
  1.2 0.0 copy-start.1
  1.2 1.0 reshape.22
  2.2 15.6 %all-to-all-start = ((bf16[256,3,256]{2,1,0:T(4,128)(2,1)}), bf16[256,3,256]{2,1,0:T(4,128)(2,1)S(1)}, u32[]{:S(2)}, u32[]{:S(2)}) async-start(bf16[256,3,256]{2,1,0:T(4,128)(2,1)} %reshape.22), calls=%async_computation | async-start | bytes 1048576 | tf_op jit(solution)/shard_map/all_to_all | solution.py:109
  17.9 0.0 copy-done.1
  17.9 0.2 copy.24
  18.1 1.0 reshape.24
  19.1 20.2 %all-to-all-done = bf16[256,3,256]{2,1,0:T(4,128)(2,1)S(1)} async-done(((bf16[256,3,256]{2,1,0:T(4,128)(2,1)}), bf16[256,3,256]{2,1,0:T(4,128)(2,1)S(1)}, u32[]{:S(2)}, u32[]{:S(2)}) %all-to-all-start) | async-done | bytes 393248 | tf_op jit(solution)/shard_map/all_to_all | solution.py:109
  39.3 5.4 %all-to-all-start.1 = ((bf16[256,3,256]{2,1,0:T(4,128)(2,1)}), bf16[256,3,256]{2,1,0:T(4,128)(2,1)S(1)}, u32[]{:S(2)}, u32[]{:S(2)}) async-start(bf16[256,3,256]{2,1,0:T(4,128)(2,1)} %reshape.24), calls=%async_computation.1 | async-start | bytes 1048576 | tf_op jit(solution)/shard_map/all_to_all | solution.py:109
  44.7 0.0 copy-done
  44.7 0.1 dynamic-slice_bitcast_fusion
  44.8 0.1 copy.27
  44.9 1.3 %constant_dynamic-slice_fusion.gain_ref = f32[2,3]{1,0:T(2,128)} fusion(f32[2,768]{1,0:T(2,128)} %param.12, s32[]{:T(128)S(6)} %select_n.4), kind=kLoop, calls=%fused_computation.5 | loop fusion | bytes 52 | tf_op jit(solution)/shard_map/dynamic_slice | solution.py:105
  46.3 0.6 pad_convert_fusion.taps_ref
  46.9 0.8 copy.40
  47.7 18.5 %all-to-all-done.1 = bf16[256,3,256]{2,1,0:T(4,128)(2,1)S(1)} async-done(((bf16[256,3,256]{2,1,0:T(4,128)(2,1)}), bf16[256,3,256]{2,1,0:T(4,128)(2,1)S(1)}, u32[]{:S(2)}, u32[]{:S(2)}) %all-to-all-start.1) | async-done | bytes 393248 | tf_op jit(solution)/shard_map/all_to_all | solution.py:109
  66.2 0.8 copy.39
  67.1 9.1 %shard_map.91 = bf16[2,3,128,256]{3,2,1,0:T(8,128)(2,1)} custom-call(bf16[2,3,128,256]{3,2,1,0:T(8,128)(2,1)} %bitcast.25, bf16[2,3,128,256]{3,2,1,0:T(8,128)(2,1)} %bitcast.26, f32[6,256]{1,0:T(8,128)} %pad_convert_fusion.taps_ref, f32[2,3]{1,0:T(2,128)} %constant_dynamic-slice_fusion.gain_ref, bf16[288,128]{1,0:T(8,128)(2,1)} %constant.30.clone.rf_ref, ...), custom_call_target="tpu_custom_call" | custom-call | tf_op jit(solution)/shard_map/pallas_call | solution.py:117
  76.1 1.3 %copy.35 = bf16[128,2,3,256]{3,2,1,0:T(4,128)(2,1)S(1)} copy(bf16[128,2,3,256]{3,0,2,1:T(8,128)(2,1)} %bitcast.27) | data formatting | bytes 786432 | tf_op jit(solution)/shard_map/reshape | solution.py:125
  77.5 26.6 %all_to_all.15 = bf16[256,3,256]{2,1,0:T(4,128)(2,1)S(1)} all-to-all(bf16[256,3,256]{2,1,0:T(4,128)(2,1)S(1)} %bitcast.24), channel_id=1, replica_groups=mesh['segment'=2,'seq'=128] {'seq','segment'}, dimensions={0} | all-to-all | bytes 786432 | tf_op jit(solution)/shard_map/all_to_all | solution.py:126
  104.1 0.3 reshape.27
  104.4 0.9 copy.30
  (2 shorter events, 0.1 us)
Async XLA Ops:
  0.0 44.7 %copy-start = (bf16[2,128,768]{2,1,0:T(8,128)(2,1)S(1)}, bf16[2,128,768]{2,1,0:T(8,128)(2,1)}, u32[]{:S(2)}) copy-start(bf16[2,128,768]{2,1,0:T(8,128)(2,1)} %param.10) | copy-start | bytes 1179652
  1.2 16.6 %copy-start.1 = (f32[1,256,768]{2,1,0:T(8,128)S(1)}, f32[1,256,768]{2,1,0:T(8,128)}, u32[]{:S(2)}) copy-start(f32[1,256,768]{2,1,0:T(8,128)} %param.11) | copy-start | bytes 2359300
  2.2 37.1 %all-to-all-start = ((bf16[256,3,256]{2,1,0:T(4,128)(2,1)}), bf16[256,3,256]{2,1,0:T(4,128)(2,1)S(1)}, u32[]{:S(2)}, u32[]{:S(2)}) async-start(bf16[256,3,256]{2,1,0:T(4,128)(2,1)} %reshape.22), calls=%async_computation | async-start | bytes 1048576 | tf_op jit(solution)/shard_map/all_to_all | solution.py:109
  39.3 27.0 %all-to-all-start.1 = ((bf16[256,3,256]{2,1,0:T(4,128)(2,1)}), bf16[256,3,256]{2,1,0:T(4,128)(2,1)S(1)}, u32[]{:S(2)}, u32[]{:S(2)}) async-start(bf16[256,3,256]{2,1,0:T(4,128)(2,1)} %reshape.24), calls=%async_computation.1 | async-start | bytes 1048576 | tf_op jit(solution)/shard_map/all_to_all | solution.py:109
where the time goes:
time: 106 us; the launch traced here: 105 us
  waiting for transfers between devices  38.7 us (37%)
  blocking collectives  26.6 us (25%)
  starting transfers between devices  21.1 us (20%)
  local copies, waits for them, and re-layouts  9.13 us (9%)
  Pallas kernels  9.07 us (9%)
    all_to_all x2, waiting for transfers between devices, outward(): got = lax.all_to_all(turned, both, 0, 0, tiled=True)  38.7 us
    all_to_all x1, blocking collectives, body(): back = lax.all_to_all(home, both, 0, 0, tiled=True)  26.6 us
    all_to_all x2, starting transfers between devices, outward(): got = lax.all_to_all(turned, both, 0, 0, tiled=True)  21.1 us
    pallas_call x1, Pallas kernels, body(): pl.pallas_call(functools.partial(filter_kernel, scale), out_shape=jax.Sha...  9.07 us
  transfers between devices with their start and end apart: 2, of which 2 were waited for; matrix products, arithmetic and copies ran while one was open for 4% of the time, Pallas kernels for 0%

commit v1 on v0

v1 whole, which is shorter than its diff:
```python
import functools
import math

import jax
import jax.numpy as jnp
import numpy as np
from jax import lax
from jax.experimental import pallas as pl
from jax.experimental.pallas import tpu as pltpu
from jax.sharding import PartitionSpec as P

MESH = pl.DeviceIdType.MESH
COLS = 128


def tables(rows, cols):
    half = rows // 2
    kept = (half + 1 + 15) // 16 * 16
    k1 = np.arange(kept)
    live = (k1 <= half).astype(np.float64)
    a = np.arange(half)
    ph = 2.0 * np.pi * ((k1[:, None] * a[None, :]) % rows) / rows
    row_fwd = np.concatenate([np.cos(ph) * live[:, None], -np.sin(ph) * live[:, None]], 0)
    weight = live * np.where((k1 == 0) | (k1 == half), 1.0, 2.0)
    row_back = np.concatenate([(np.cos(ph) * weight[:, None]).T, (-np.sin(ph) * weight[:, None]).T], 1)
    b = np.arange(cols)
    pc = 2.0 * np.pi * ((b[:, None] * b[None, :]) % cols) / cols
    c, s = np.cos(pc), np.sin(pc)
    col_fwd = np.block([[c, -s], [s, c]])
    col_back = np.block([[c, s], [-s, c]])
    tw = 2.0 * np.pi * ((k1[:, None] * b[None, :]) % (rows * cols)) / (rows * cols)
    bf = lambda x: jnp.asarray(x, jnp.bfloat16)
    return (
        bf(row_fwd), bf(row_back), bf(col_fwd), bf(col_back),
        jnp.asarray(np.stack([np.cos(tw), np.sin(tw)]), jnp.float32),
    )


def dot(a, b):
    return jnp.dot(a, b, preferred_element_type=jnp.float32)


def kernel(scale, kept, x_ref, f_ref, taps_ref, gain_ref, rf_ref, rb_ref, cf_ref, cb_ref, tw_ref,
           out_ref, x_in, f_in, y_out, y_in, spec, send_sem, f_sem, x_sem, y_sem):
    channels = taps_ref.shape[0] // 2
    seqs = x_in.shape[2]
    rows, cols = 2 * seqs, x_in.shape[4]
    q, s = lax.axis_index("seq"), lax.axis_index("segment")
    zs = [lax.rem(q + d, 8) for d in range(8)]
    cores = [s, 1 - s]
    mine = q * 2 + s

    def everyone(copy_to, some_cores):
        def group(xy, is_first):
            for dz in range(8):
                for core in some_cores:
                    seq, core_now = xy + zs[dz], cores[core]
                    if not (is_first and dz == 0 and core == 0):
                        copy_to(seq, core_now)

        x, y = q // 32, lax.rem(q // 8, 4)
        group(q - zs[0], True)

        def step(g, carry):
            group(lax.rem(x + g // 4, 4) * 32 + lax.rem(y + lax.rem(g, 4), 4) * 8, False)
            return carry

        lax.fori_loop(1, 16, step, 0)

    def send_in(from_ref, to_ref, sent_sem, sem):
        pltpu.make_async_copy(from_ref.at[mine], to_ref.at[s, :, q], sem).start()
        everyone(
            lambda seq, core: pltpu.make_async_remote_copy(
                from_ref.at[seq * 2 + core], to_ref.at[s, :, q], sent_sem, sem,
                device_id={"segment": core, "seq": seq}, device_id_type=MESH,
            ).start(),
            (0, 1),
        )

    def send_out(section):
        def go(seq, core):
            pltpu.make_async_remote_copy(
                y_out.at[section, :, seq], y_in.at[mine], send_sem.at[2], y_sem,
                device_id={"segment": section, "seq": seq}, device_id_type=MESH,
            ).start()

        @pl.when(s == section)
        def _():
            pltpu.make_async_copy(y_out.at[section, :, q], y_in.at[mine], y_sem).start()
            everyone(go, (0,))

        @pl.when(s != section)
        def _():
            everyone(go, (1,))

    send_in(f_ref, f_in, send_sem.at[0], f_sem)
    send_in(x_ref, x_in, send_sem.at[1], x_sem)

    b_in = lax.broadcasted_iota(jnp.int32, (cols, cols), 0)
    b_out = lax.broadcasted_iota(jnp.int32, (cols, cols), 1)
    top = lax.broadcasted_iota(jnp.int32, (rows, cols), 0) == 0

    def spectrum(grids):
        first = dot(rf_ref[...], jnp.concatenate(grids, 1))
        turned = []
        for c in range(len(grids)):
            re, im = first[:kept, c * cols:(c + 1) * cols], first[kept:, c * cols:(c + 1) * cols]
            cosine, sine = tw_ref[0], tw_ref[1]
            turned.append(jnp.concatenate(
                [re * cosine + im * sine, im * cosine - re * sine], 1
            ).astype(jnp.bfloat16))
        return [dot(t, cf_ref[...]) for t in turned]

    def inverse(products):
        turned = []
        for product in products:
            back = dot(product, cb_ref[...])
            re, im = back[:, :cols], back[:, cols:]
            cosine, sine = tw_ref[0], tw_ref[1]
            turned.append(jnp.concatenate(
                [re * cosine - im * sine, re * sine + im * cosine], 0
            ).astype(jnp.bfloat16))
        y = dot(rb_ref[...], jnp.concatenate(turned, 1)) * scale
        return [y[:, c * cols:(c + 1) * cols] for c in range(len(products))]

    def short(grid, taps):
        circ = pltpu.roll(jnp.broadcast_to(taps, (cols, cols)), 0, 1, stride=1, stride_axis=0)
        both = jnp.concatenate(
            [jnp.where(b_out >= b_in, circ, 0.0), jnp.where(b_out < b_in, circ, 0.0)], 0
        ).astype(jnp.bfloat16)
        earlier = jnp.where(top, 0.0, pltpu.roll(grid, 1, 0))
        return dot(jnp.concatenate([grid, earlier], 1).astype(jnp.bfloat16), both).astype(jnp.bfloat16)

    pltpu.make_async_copy(f_in, f_in, f_sem).wait()
    for section in range(2):
        got = spectrum([f_in[section, c].reshape(rows, cols) for c in range(channels)])
        for c in range(channels):
            spec[section, c] = got[c]

    pltpu.make_async_copy(x_in, x_in, x_sem).wait()
    previous = None
    for section in range(2):
        zs_now = []
        for c in range(channels):
            grid = x_in[section, c].reshape(rows, cols).astype(jnp.float32)
            if section:
                grid = (previous[c] * grid).astype(jnp.bfloat16).astype(jnp.float32)
            zs_now.append(short(grid, taps_ref[section * channels + c][None, :]))
        products = []
        for c, signal in enumerate(spectrum(zs_now)):
            other = spec[section, c]
            ar, ai = signal[:, :cols], signal[:, cols:]
            hr, hi = other[:, :cols], other[:, cols:]
            products.append(
                jnp.concatenate([ar * hr - ai * hi, ar * hi + ai * hr], 1).astype(jnp.bfloat16)
            )
        previous = []
        for c, long in enumerate(inverse(products)):
            y = (
                long.astype(jnp.bfloat16).astype(jnp.float32)
                + gain_ref[section, c] * zs_now[c].astype(jnp.float32)
            ).astype(jnp.bfloat16)
            previous.append(y.astype(jnp.float32))
            y_out[section, c] = y.reshape(seqs, 2, cols)
        send_out(section)

    pltpu.make_async_copy(y_in, y_in, y_sem).wait()
    out_ref[...] = y_in[...]
    sent = x_ref.shape[0] - 1
    for i, ref in enumerate((f_ref, x_ref, y_in)):
        part = ref.at[pl.ds(0, sent)]
        pltpu.make_async_copy(part, part, send_sem.at[i]).wait()


def body(activations, short_filters, long_filters, skip_gain):
    tokens, width = activations.shape[1:]
    segs, seqs = lax.axis_size("segment"), lax.axis_size("seq")
    parts = segs * seqs
    mine = width // parts
    cols = COLS
    per = tokens // cols
    rows = 2 * per * seqs
    first = (lax.axis_index("seq") * segs + lax.axis_index("segment")) * mine
    taps = lax.dynamic_slice_in_dim(short_filters, first, mine, 2)
    taps = jnp.swapaxes(taps, 1, 2).reshape(2 * mine, -1).astype(jnp.float32)
    gains = lax.dynamic_slice_in_dim(skip_gain, first, mine, 1)

    def by_channel(block):
        return block.T.reshape(parts, mine, per, cols)

    scale = 1.0 / (rows * cols * math.sqrt(rows * cols // 2))
    tabs = tables(rows, cols)
    kept = tabs[4].shape[1]
    vm = pl.BlockSpec(memory_space=pltpu.VMEM)
    sm = pl.BlockSpec(memory_space=pltpu.SMEM)
    grid = pltpu.VMEM((2, mine, seqs, per, cols), jnp.bfloat16)
    chunks = pltpu.VMEM((parts, mine, per, cols), jnp.bfloat16)
    home = pl.pallas_call(
        functools.partial(kernel, scale, kept),
        out_shape=jax.ShapeDtypeStruct((parts, mine, per, cols), jnp.bfloat16),
        in_specs=[vm, vm, vm, sm, vm, vm, vm, vm, vm],
        out_specs=vm,
        scratch_shapes=[
            grid, grid, grid, chunks,
            pltpu.VMEM((2, mine, kept, 2 * cols), jnp.float32),
            pltpu.SemaphoreType.DMA((3,)), pltpu.SemaphoreType.DMA, pltpu.SemaphoreType.DMA,
            pltpu.SemaphoreType.DMA,
        ],
        compiler_params=pltpu.CompilerParams(
            vmem_limit_bytes=56 * 1024 * 1024, has_side_effects=True
        ),
    )(
        by_channel(activations[0]), by_channel(long_filters[0].astype(jnp.bfloat16)),
        taps, gains, *tabs,
    )
    return home.reshape(width, tokens).T[None]


def solution(mesh):
    return jax.shard_map(
        body,
        mesh=mesh,
        in_specs=(P("segment", "seq", None), P(), P("segment", "seq", None), P()),
        out_specs=P("segment", "seq", None),
        check_vma=False,
    )
```

time: 106 us -> 65.5 us (0.62)
  Pallas kernels: 9.07 us -> 57.1 us
  waiting for transfers between devices: 38.7 us -> 0 us
  blocking collectives: 26.6 us -> 0 us
  starting transfers between devices: 21.1 us -> 0 us
  local copies, waits for them, and re-layouts: 9.13 us -> 7.1 us
    pallas_call x1, Pallas kernels: 9.07 us -> 57.1 us  [body(): pl.pallas_call(functools.partial(kernel, scale, kept), out_shape=jax.Shap...]
    all_to_all x2 -> x0, waiting for transfers between devices: 38.7 us -> none  [outward(): got = lax.all_to_all(turned, both, 0, 0, tiled=True)]
    all_to_all x1 -> x0, blocking collectives: 26.6 us -> none  [body(): back = lax.all_to_all(home, both, 0, 0, tiled=True)]
    all_to_all x2 -> x0, starting transfers between devices: 21.1 us -> none  [outward(): got = lax.all_to_all(turned, both, 0, 0, tiled=True)]
    reshape x6 -> x3, local copies, waits for them, and re-layouts: 5.27 us -> 2.61 us  [the longest x2 1.68 us: by_channel(): return block.T.reshape(parts, mine, per, cols)]
    unnamed x4 -> x5, local copies, waits for them, and re-layouts: 0.01 us -> 1.75 us
  transfers between devices with their start and end apart: 2 -> 0, of which waited for: 2 -> 0; matrix products, arithmetic and copies ran while one was open for 4% -> 0% of each run, Pallas kernels for 0% -> 0%
where the time goes in v1:
time: 65.5 us; the launch traced here: 65.3 us
  Pallas kernels  57.1 us (87%)
  local copies, waits for them, and re-layouts  7.1 us (11%)
  other arithmetic  1.03 us (2%)
    pallas_call x1, Pallas kernels, body(): pl.pallas_call(functools.partial(kernel, scale, kept), out_shape=jax.Shap...  57.1 us
    unnamed x5, local copies, waits for them, and re-layouts  1.75 us
    reshape x2, local copies, waits for them, and re-layouts, by_channel(): return block.T.reshape(parts, mine, per, cols)  1.68 us
    transpose x2, local copies, waits for them, and re-layouts, by_channel(): return block.T.reshape(parts, mine, per, cols)  1.41 us

profile of v1, /device:TPU:1, one launch (start us, length us, event | category | flops | bytes accessed | tf_op | source)
XLA Modules:
  0.0 65.3 jit_solution(14387189641240576602)
XLA Ops:
  0.0 0.0 copy-start
  0.0 0.7 %copy-done = f32[2,768]{1,0:T(2,128)S(1)} copy-done((f32[2,768]{1,0:T(2,128)S(1)}, f32[2,768]{1,0:T(2,128)}, u32[]{:S(2)}) %copy-start) | copy-done | bytes 6168
  0.7 0.6 constant_dynamic-slice_fusion.gain_ref
  1.3 1.0 %convert_bitcast_fusion.1 = f32[2,3,128]{1,2,0:T(8,128)S(1)} fusion(bf16[2,128,768]{2,1,0:T(8,128)(2,1)} %param.10, s32[]{:T(128)S(6)} %select_n.4), kind=kLoop, calls=%fused_computation.2 | loop fusion | flops 768 | bytes 4612 | tf_op jit(solution)/shard_map/convert_element_type | solution.py:185
  2.3 0.1 copy.16
  2.4 0.6 reshape.16.taps_ref
  3.0 0.0 copy-start.1
  3.0 1.2 %copy.14 = bf16[768,256]{1,0:T(8,128)(2,1)S(1)} copy(bf16[768,256]{0,1:T(8,128)(2,1)} %bitcast.19) | data formatting | bytes 786432 | tf_op jit(solution)/shard_map/transpose | solution.py:189
  4.3 0.8 %reshape.13.x_ref = bf16[256,3,2,128]{3,2,1,0:T(2,128)(2,1)} reshape(bf16[768,256]{1,0:T(8,128)(2,1)S(1)} %copy.14) | data formatting | bytes 786432 | tf_op jit(solution)/shard_map/reshape | solution.py:189
  5.1 0.0 copy-done.1
  5.2 0.2 copy.15
  5.3 0.8 %reshape.14.f_ref = bf16[256,3,2,128]{3,2,1,0:T(2,128)(2,1)} reshape(bf16[768,256]{1,0:T(8,128)(2,1)S(1)} %copy.15) | data formatting | bytes 786432 | tf_op jit(solution)/shard_map/reshape | solution.py:189
  6.2 57.1 %shard_map.91 = bf16[256,3,2,128]{3,2,1,0:T(2,128)(2,1)} custom-call(bf16[256,3,2,128]{3,2,1,0:T(2,128)(2,1)} %reshape.13.x_ref, bf16[256,3,2,128]{3,2,1,0:T(2,128)(2,1)} %reshape.14.f_ref, f32[6,128]{1,0:T(8,128)} %reshape.16.taps_ref, f32[2,3]{1,0:T(2,128)} %constant_dynamic-slice_fusion.gain_ref, bf16[544,256]{1,0:T(8,128)(2,1)} %constant.27.clone.rf_ref, ...), custom_call_target="tpu_custom_call" | custom-call | tf_op jit(solution)/shard_map/pallas_call | solution.py:198
  63.3 1.1 %copy.20 = bf16[96,8,2,128]{3,1,2,0:T(8,128)(2,1)S(1)} copy(bf16[96,8,2,128]{3,2,1,0:T(2,128)(2,1)} %bitcast.18) | data formatting | bytes 786432
  64.3 0.9 %copy.17 = bf16[768,256]{0,1:T(8,128)(2,1)} copy(bf16[768,256]{1,0:T(8,128)(2,1)S(1)} %bitcast.17) | data formatting | bytes 786432 | tf_op jit(solution)/shard_map/reshape | solution.py:216
  (1 shorter events, 0.0 us)
Async XLA Ops:
  0.0 0.7 %copy-start = (f32[2,768]{1,0:T(2,128)S(1)}, f32[2,768]{1,0:T(2,128)}, u32[]{:S(2)}) copy-start(f32[2,768]{1,0:T(2,128)} %param.12) | copy-start | bytes 18436
  3.0 2.1 %copy-start.1 = (f32[1,256,768]{2,1,0:T(8,128)S(1)}, f32[1,256,768]{2,1,0:T(8,128)}, u32[]{:S(2)}) copy-start(f32[1,256,768]{2,1,0:T(8,128)} %param.11) | copy-start | bytes 2359300

commit v2 on v1

v2 whole, which is shorter than its diff:
```python
import functools
import math

import jax
import jax.numpy as jnp
import numpy as np
from jax import lax
from jax.experimental import pallas as pl
from jax.experimental.pallas import tpu as pltpu
from jax.sharding import PartitionSpec as P

MESH = pl.DeviceIdType.MESH
COLS = 128


def tables(rows, cols):
    half = rows // 2
    kept = (half + 1 + 15) // 16 * 16
    k1 = np.arange(kept)
    live = (k1 <= half).astype(np.float64)
    a = np.arange(half)
    ph = 2.0 * np.pi * ((k1[:, None] * a[None, :]) % rows) / rows
    row_fwd = np.concatenate([np.cos(ph) * live[:, None], -np.sin(ph) * live[:, None]], 0)
    weight = live * np.where((k1 == 0) | (k1 == half), 1.0, 2.0)
    row_back = np.concatenate([(np.cos(ph) * weight[:, None]).T, (-np.sin(ph) * weight[:, None]).T], 1)
    b = np.arange(cols)
    pc = 2.0 * np.pi * ((b[:, None] * b[None, :]) % cols) / cols
    c, s = np.cos(pc), np.sin(pc)
    col_fwd = np.block([[c, -s], [s, c]])
    col_back = np.block([[c, s], [-s, c]])
    tw = 2.0 * np.pi * ((k1[:, None] * b[None, :]) % (rows * cols)) / (rows * cols)
    bf = lambda x: jnp.asarray(x, jnp.bfloat16)
    return (
        bf(row_fwd), bf(row_back), bf(col_fwd), bf(col_back),
        jnp.asarray(np.stack([np.cos(tw), np.sin(tw)]), jnp.float32),
    )


def dot(a, b):
    return jnp.dot(a, b, preferred_element_type=jnp.float32)


def far_first(sizes):
    offsets = [(x, y, z) for x in range(sizes[0]) for y in range(sizes[1]) for z in range(sizes[2])]
    hops = lambda o: sum(min(d, n - d) for d, n in zip(o, sizes))
    return sorted(offsets, key=lambda o: (-hops(o), o))


def nt(a, b):
    return lax.dot_general(a, b, (((1,), (1,)), ((), ())), preferred_element_type=jnp.float32)


def tn(a, b):
    return lax.dot_general(a, b, (((0,), (0,)), ((), ())), preferred_element_type=jnp.float32)


def kernel(scale, kept, x_hbm, f_hbm, taps_hbm, gain_ref, rf_hbm, rb_hbm, cf_hbm, cb_hbm, tw_hbm,
           out_ref, x_raw, f_raw, taps_ref, rf_ref, rb_ref, cf_ref, cb_ref, tw_ref,
           both_send, both_in, y_out, y_in, spec,
           load_sem, send_sem, in_sem, y_sem):
    x_send, f_send = both_send.at[0], both_send.at[1]
    x_in, f_in = both_in.at[0], both_in.at[1]
    channels, seqs, cols = x_in.shape[1], x_in.shape[2], x_in.shape[4]
    width = x_send.shape[0]
    rows = 2 * seqs
    q, s = lax.axis_index("seq"), lax.axis_index("segment")
    mine = q * 2 + s
    xs = [lax.rem(q // 32 + d, 4) * 32 for d in range(4)]
    ys = [lax.rem(q // 8 + d, 4) * 8 for d in range(4)]
    zs = [lax.rem(q + d, 8) for d in range(8)]
    others = far_first((4, 4, 8))

    def seq_at(offset):
        return xs[offset[0]] + ys[offset[1]] + zs[offset[2]]

    def everyone(act):
        for offset in others:
            seq = seq_at(offset)
            act(seq, 1 - s)
            if any(offset):
                act(seq, s)

    loads = []
    for k, (a, b) in enumerate([
        (x_hbm, x_raw), (f_hbm, f_raw), (rf_hbm, rf_ref), (cf_hbm, cf_ref), (tw_hbm, tw_ref),
        (taps_hbm, taps_ref), (rb_hbm, rb_ref), (cb_hbm, cb_ref),
    ]):
        copy = pltpu.make_async_copy(a, b, load_sem.at[k])
        copy.start()
        loads.append(copy)

    barrier = pltpu.get_barrier_semaphore()
    everyone(lambda seq, core: pl.semaphore_signal(
        barrier, inc=1, device_id={"segment": core, "seq": seq}, device_id_type=MESH))

    weave = lax.broadcasted_iota(jnp.int32, (2 * cols, 2 * cols), 0)
    lane = lax.broadcasted_iota(jnp.int32, (2 * cols, 2 * cols), 1)
    weave = (lane == lax.rem(weave, 2) * cols + weave // 2).astype(jnp.float32).astype(jnp.bfloat16)

    def by_channel(raw, to_ref):
        for k in range(width // cols):
            block = raw[:, k * cols:(k + 1) * cols].astype(jnp.bfloat16)
            block = jnp.concatenate([block[:cols], block[cols:]], 1)
            woven = nt(weave, block).astype(jnp.bfloat16)
            to_ref[k * cols:(k + 1) * cols] = woven.reshape(cols, 2, cols)

    loads[1].wait()
    by_channel(f_raw, f_send)
    loads[0].wait()
    by_channel(x_raw, x_send)
    pl.semaphore_wait(barrier, 2 * seqs - 1)

    to_ref = both_in.at[:, s, :, q]
    everyone(lambda seq, core: pltpu.make_async_remote_copy(
        both_send.at[:, pl.ds((seq * 2 + core) * channels, channels)], to_ref,
        send_sem.at[0], in_sem, device_id={"segment": core, "seq": seq}, device_id_type=MESH,
    ).start())
    pltpu.make_async_copy(
        both_send.at[:, pl.ds(mine * channels, channels)], to_ref, in_sem
    ).start()

    def send_out(section):
        to_ref = y_in.at[pl.ds(mine * channels, channels)]

        def go(seq):
            pltpu.make_async_remote_copy(
                y_out.at[section, :, seq], to_ref, send_sem.at[1], y_sem,
                device_id={"segment": section, "seq": seq}, device_id_type=MESH,
            ).start()

        for offset in others:
            if any(offset):
                go(seq_at(offset))

        @pl.when(s == section)
        def _():
            pltpu.make_async_copy(y_out.at[section, :, q], to_ref, y_sem).start()

        @pl.when(s != section)
        def _():
            go(q)

    for copy in loads[2:]:
        copy.wait()
    first = mine * channels
    pick_c = lax.broadcasted_iota(jnp.int32, (16, width), 0)
    pick_l = lax.broadcasted_iota(jnp.int32, (16, width), 1)
    pick = (pick_l == first + pick_c).astype(jnp.float32)
    taps = [nt(pick.astype(jnp.bfloat16), taps_ref[section]) for section in range(2)]
    gains = [
        jnp.sum(jnp.where(pick > 0, gain_ref[section][None, :], 0.0), 1, keepdims=True)
        for section in range(2)
    ]

    b_in = lax.broadcasted_iota(jnp.int32, (cols, cols), 0)
    b_out = lax.broadcasted_iota(jnp.int32, (cols, cols), 1)
    top = lax.broadcasted_iota(jnp.int32, (rows, cols), 0) == 0

    def spectrum(grids):
        first = dot(rf_ref[...], jnp.concatenate(grids, 1))
        turned = []
        for c in range(len(grids)):
            re, im = first[:kept, c * cols:(c + 1) * cols], first[kept:, c * cols:(c + 1) * cols]
            cosine, sine = tw_ref[0], tw_ref[1]
            turned.append(jnp.concatenate(
                [re * cosine + im * sine, im * cosine - re * sine], 1
            ).astype(jnp.bfloat16))
        return [dot(t, cf_ref[...]) for t in turned]

    def inverse(products):
        turned = []
        for product in products:
            back = dot(product, cb_ref[...])
            re, im = back[:, :cols], back[:, cols:]
            cosine, sine = tw_ref[0], tw_ref[1]
            turned.append(jnp.concatenate(
                [re * cosine - im * sine, re * sine + im * cosine], 0
            ).astype(jnp.bfloat16))
        y = dot(rb_ref[...], jnp.concatenate(turned, 1)) * scale
        return [y[:, c * cols:(c + 1) * cols] for c in range(len(products))]

    def short(grid, taps):
        circ = pltpu.roll(jnp.broadcast_to(taps, (cols, cols)), 0, 1, stride=1, stride_axis=0)
        both = jnp.concatenate(
            [jnp.where(b_out >= b_in, circ, 0.0), jnp.where(b_out < b_in, circ, 0.0)], 0
        ).astype(jnp.bfloat16)
        earlier = jnp.where(top, 0.0, pltpu.roll(grid, 1, 0))
        return dot(jnp.concatenate([grid, earlier], 1).astype(jnp.bfloat16), both).astype(jnp.bfloat16)

    pltpu.make_async_copy(both_in, both_in, in_sem).wait()
    for section in range(2):
        got = spectrum([f_in[section, c].reshape(rows, cols) for c in range(channels)])
        for c in range(channels):
            spec[section, c] = got[c]

    previous = None
    for section in range(2):
        zs_now = []
        for c in range(channels):
            grid = x_in[section, c].reshape(rows, cols).astype(jnp.float32)
            if section:
                grid = (previous[c] * grid).astype(jnp.bfloat16).astype(jnp.float32)
            zs_now.append(short(grid, taps[section][c:c + 1]))
        products = []
        for c, signal in enumerate(spectrum(zs_now)):
            other = spec[section, c]
            ar, ai = signal[:, :cols], signal[:, cols:]
            hr, hi = other[:, :cols], other[:, cols:]
            products.append(
                jnp.concatenate([ar * hr - ai * hi, ar * hi + ai * hr], 1).astype(jnp.bfloat16)
            )
        previous = []
        for c, long in enumerate(inverse(products)):
            y = (
                long.astype(jnp.bfloat16).astype(jnp.float32)
                + gains[section][c:c + 1] * zs_now[c].astype(jnp.float32)
            ).astype(jnp.bfloat16)
            previous.append(y.astype(jnp.float32))
            y_out[section, c] = y.reshape(seqs, 2, cols)
        send_out(section)

    pltpu.make_async_copy(y_in, y_in, y_sem).wait()
    for k in range(width // cols):
        block = tn(y_in[k * cols:(k + 1) * cols].reshape(2 * cols, cols), weave).astype(jnp.bfloat16)
        out_ref[:cols, k * cols:(k + 1) * cols] = block[:, :cols]
        out_ref[cols:, k * cols:(k + 1) * cols] = block[:, cols:]
    part = both_send.at[:, pl.ds(0, width - channels)]
    pltpu.make_async_copy(part, part, send_sem.at[0]).wait()
    part = y_in.at[pl.ds(0, width - channels)]
    pltpu.make_async_copy(part, part, send_sem.at[1]).wait()


def body(activations, short_filters, long_filters, skip_gain):
    tokens, width = activations.shape[1:]
    segs, seqs = lax.axis_size("segment"), lax.axis_size("seq")
    mine = width // (segs * seqs)
    cols = COLS
    per = tokens // cols
    rows = 2 * per * seqs
    scale = 1.0 / (rows * cols * math.sqrt(rows * cols // 2))
    tabs = tables(rows, cols)
    kept = tabs[4].shape[1]
    vm = pl.BlockSpec(memory_space=pltpu.VMEM)
    far = pl.BlockSpec(memory_space=pl.ANY)
    grid = (2, mine, seqs, per, cols)
    chunks = (width, per, cols)
    vmem = lambda *shape: pltpu.VMEM(shape, jnp.bfloat16)
    like = lambda a: pltpu.VMEM(a.shape, a.dtype)
    x, f = activations[0], long_filters[0]
    dma = pltpu.SemaphoreType.DMA
    out = pl.pallas_call(
        functools.partial(kernel, scale, kept),
        out_shape=jax.ShapeDtypeStruct((tokens, width), jnp.bfloat16),
        in_specs=[far, far, far, vm, far, far, far, far, far],
        out_specs=vm,
        scratch_shapes=[
            like(x), like(f), like(short_filters), *[like(t) for t in tabs],
            vmem(2, *chunks), vmem(2, *grid), vmem(*grid), vmem(*chunks),
            pltpu.VMEM((2, mine, kept, 2 * cols), jnp.float32),
            dma((8,)), dma((2,)), dma, dma,
        ],
        compiler_params=pltpu.CompilerParams(
            vmem_limit_bytes=60 * 1024 * 1024, has_side_effects=True, collective_id=0
        ),
    )(x, f, short_filters, skip_gain, *tabs)
    return out[None]


def solution(mesh):
    return jax.shard_map(
        body,
        mesh=mesh,
        in_specs=(P("segment", "seq", None), P(), P("segment", "seq", None), P()),
        out_specs=P("segment", "seq", None),
        check_vma=False,
    )
```

time: 65.5 us -> 51.9 us (0.79)
  Pallas kernels: 57.1 us -> 50 us
  local copies, waits for them, and re-layouts: 7.1 us -> 1.77 us
  other arithmetic: 1.03 us -> 0 us
    pallas_call x1, Pallas kernels: 57.1 us -> 50 us  [body(): pl.pallas_call(functools.partial(kernel, scale, kept), out_shape=jax.Shap...]
    reshape x3 -> x0, local copies, waits for them, and re-layouts: 2.61 us -> none  [the longest x2 1.68 us: by_channel(): return block.T.reshape(parts, mine, per, cols)]
    transpose x2 -> x0, local copies, waits for them, and re-layouts: 1.41 us -> none  [by_channel(): return block.T.reshape(parts, mine, per, cols)]
    convert_element_type x1 -> x0, other arithmetic: 0.99 us -> none  [body(): taps = jnp.swapaxes(taps, 1, 2).reshape(2 * mine, -1).astype(jnp.float32)]
    convert_element_type x2 -> x0, local copies, waits for them, and re-layouts: 0.69 us -> none  [body(): taps = jnp.swapaxes(taps, 1, 2).reshape(2 * mine, -1).astype(jnp.float32)]
    unnamed x5 -> x1, local copies, waits for them, and re-layouts: 1.75 us -> 1.77 us
where the time goes in v2:
time: 51.9 us; the launch traced here: 51.8 us
  Pallas kernels  50 us (96%)
  local copies, waits for them, and re-layouts  1.77 us (3%)
    pallas_call x1, Pallas kernels, body(): pl.pallas_call(functools.partial(kernel, scale, kept), out_shape=jax.Shap...  50 us
    unnamed x1, local copies, waits for them, and re-layouts  1.77 us

profile of v2, /device:TPU:1, one launch (start us, length us, event | category | flops | bytes accessed | tf_op | source)
XLA Modules:
  0.0 51.8 jit_solution(5849001090205670511)
XLA Ops:
  0.0 50.0 %shard_map.91 = bf16[256,768]{1,0:T(8,128)(2,1)} custom-call(bf16[256,768]{1,0:T(8,128)(2,1)} %bitcast.5, f32[256,768]{1,0:T(8,128)} %bitcast.4, bf16[2,128,768]{2,1,0:T(8,128)(2,1)} %taps_hbm.1, f32[2,768]{1,0:T(2,128)} %gain_ref.1, bf16[544,256]{1,0:T(8,128)(2,1)} %constant.10.clone.rf_hbm, bf16[256,544]{1,0:T(8,128)(2,1)} %constant.11.clone.rb_hbm, ...), custom_call_target="tpu_custom_call" | custom-call | tf_op jit(solution)/shard_map/pallas_call | solution.py:251
  50.0 1.8 %copy.11 = bf16[1,256,768]{2,1,0:T(8,128)(2,1)} copy(bf16[1,256,768]{2,1,0:T(8,128)(2,1)} %bitcast.3) | data formatting | bytes 786432

commit v3 on v2

--- a/solution.py
+++ b/solution.py
@@ -54,10 +54,10 @@
     return lax.dot_general(a, b, (((0,), (0,)), ((), ())), preferred_element_type=jnp.float32)
 
 
-def kernel(scale, kept, x_hbm, f_hbm, taps_hbm, gain_ref, rf_hbm, rb_hbm, cf_hbm, cb_hbm, tw_hbm,
-           out_ref, x_raw, f_raw, taps_ref, rf_ref, rb_ref, cf_ref, cb_ref, tw_ref,
-           both_send, both_in, y_out, y_in, spec,
-           load_sem, send_sem, in_sem, y_sem):
+def kernel(scale, kept, x_hbm, f_hbm, taps_hbm, gain_hbm, rf_hbm, rb_hbm, cf_hbm, cb_hbm, tw_hbm,
+           out_ref, x_raw, f_raw, taps_ref, gain_ref, rf_ref, rb_ref, cf_ref, cb_ref, tw_ref,
+           both_send, both_in, y_out, y_in, spec, toeplitz,
+           load_sem, send_sem, in_sems, y_sem):
     x_send, f_send = both_send.at[0], both_send.at[1]
     x_in, f_in = both_in.at[0], both_in.at[1]
     channels, seqs, cols = x_in.shape[1], x_in.shape[2], x_in.shape[4]
@@ -84,6 +84,7 @@
     for k, (a, b) in enumerate([
         (x_hbm, x_raw), (f_hbm, f_raw), (rf_hbm, rf_ref), (cf_hbm, cf_ref), (tw_hbm, tw_ref),
         (taps_hbm, taps_ref), (rb_hbm, rb_ref), (cb_hbm, cb_ref),
+        (gain_hbm, gain_ref),
     ]):
         copy = pltpu.make_async_copy(a, b, load_sem.at[k])
         copy.start()
@@ -110,6 +111,7 @@
     by_channel(x_raw, x_send)
     pl.semaphore_wait(barrier, 2 * seqs - 1)
 
+    in_sem = in_sems.at[s]
     to_ref = both_in.at[:, s, :, q]
     everyone(lambda seq, core: pltpu.make_async_remote_copy(
         both_send.at[:, pl.ds((seq * 2 + core) * channels, channels)], to_ref,
@@ -179,28 +181,33 @@
         y = dot(rb_ref[...], jnp.concatenate(turned, 1)) * scale
         return [y[:, c * cols:(c + 1) * cols] for c in range(len(products))]
 
-    def short(grid, taps):
-        circ = pltpu.roll(jnp.broadcast_to(taps, (cols, cols)), 0, 1, stride=1, stride_axis=0)
-        both = jnp.concatenate(
-            [jnp.where(b_out >= b_in, circ, 0.0), jnp.where(b_out < b_in, circ, 0.0)], 0
-        ).astype(jnp.bfloat16)
+    def short(grid, section, c):
         earlier = jnp.where(top, 0.0, pltpu.roll(grid, 1, 0))
-        return dot(jnp.concatenate([grid, earlier], 1).astype(jnp.bfloat16), both).astype(jnp.bfloat16)
-
-    pltpu.make_async_copy(both_in, both_in, in_sem).wait()
+        both = jnp.concatenate([grid, earlier], 1).astype(jnp.bfloat16)
+        return dot(both, toeplitz[section, c]).astype(jnp.bfloat16)
+
     for section in range(2):
+        for c in range(channels):
+            circ = pltpu.roll(
+                jnp.broadcast_to(taps[section][c:c + 1], (cols, cols)), 0, 1, stride=1, stride_axis=0
+            )
+            toeplitz[section, c] = jnp.concatenate(
+                [jnp.where(b_out >= b_in, circ, 0.0), jnp.where(b_out < b_in, circ, 0.0)], 0
+            ).astype(jnp.bfloat16)
+
+    previous = None
+    for section in range(2):
+        part = both_in.at[:, section]
+        pltpu.make_async_copy(part, part, in_sems.at[section]).wait()
         got = spectrum([f_in[section, c].reshape(rows, cols) for c in range(channels)])
         for c in range(channels):
             spec[section, c] = got[c]
-
-    previous = None
-    for section in range(2):
         zs_now = []
         for c in range(channels):
             grid = x_in[section, c].reshape(rows, cols).astype(jnp.float32)
             if section:
                 grid = (previous[c] * grid).astype(jnp.bfloat16).astype(jnp.float32)
-            zs_now.append(short(grid, taps[section][c:c + 1]))
+            zs_now.append(short(grid, section, c))
         products = []
         for c, signal in enumerate(spectrum(zs_now)):
             other = spec[section, c]
@@ -250,17 +257,17 @@
     dma = pltpu.SemaphoreType.DMA
     out = pl.pallas_call(
         functools.partial(kernel, scale, kept),
-        out_shape=jax.ShapeDtypeStruct((tokens, width), jnp.bfloat16),
-        in_specs=[far, far, far, vm, far, far, far, far, far],
+        out_shape=pltpu.VMEM((tokens, width), jnp.bfloat16),
+        in_specs=[far] * 9,
         out_specs=vm,
         scratch_shapes=[
-            like(x), like(f), like(short_filters), *[like(t) for t in tabs],
+            like(x), like(f), like(short_filters), like(skip_gain), *[like(t) for t in tabs],
             vmem(2, *chunks), vmem(2, *grid), vmem(*grid), vmem(*chunks),
-            pltpu.VMEM((2, mine, kept, 2 * cols), jnp.float32),
-            dma((8,)), dma((2,)), dma, dma,
+            pltpu.VMEM((2, mine, kept, 2 * cols), jnp.float32), vmem(2, mine, 2 * cols, cols),
+            dma((9,)), dma((2,)), dma((2,)), dma,
         ],
         compiler_params=pltpu.CompilerParams(
-            vmem_limit_bytes=60 * 1024 * 1024, has_side_effects=True, collective_id=0
+            vmem_limit_bytes=54900 * 1024, has_side_effects=True, collective_id=0
         ),
     )(x, f, short_filters, skip_gain, *tabs)
     return out[None]

time: 51.9 us -> 49.1 us (0.946)
  Pallas kernels: 50 us -> 48.3 us
  local copies, waits for them, and re-layouts: 1.77 us -> 0.75 us
    pallas_call x1, Pallas kernels: 50 us -> 48.3 us  [body(): pl.pallas_call(functools.partial(kernel, scale, kept), out_shape=pltpu.VM...]
    unnamed x1, local copies, waits for them, and re-layouts: 1.77 us -> 0.75 us
where the time goes in v3:
time: 49.1 us; the launch traced here: 49 us
  Pallas kernels  48.3 us (98%)
  local copies, waits for them, and re-layouts  0.75 us (2%)
    pallas_call x1, Pallas kernels, body(): pl.pallas_call(functools.partial(kernel, scale, kept), out_shape=pltpu.VM...  48.3 us

profile of v3, /device:TPU:1, one launch (start us, length us, event | category | flops | bytes accessed | tf_op | source)
XLA Modules:
  0.0 49.0 jit_solution(12234224256427203017)
XLA Ops:
  0.0 48.3 %shard_map.91 = bf16[256,768]{1,0:T(8,128)(2,1)S(1)} custom-call(bf16[256,768]{1,0:T(8,128)(2,1)} %bitcast.5, f32[256,768]{1,0:T(8,128)} %bitcast.4, bf16[2,128,768]{2,1,0:T(8,128)(2,1)} %taps_hbm.1, f32[2,768]{1,0:T(2,128)} %gain_hbm.1, bf16[544,256]{1,0:T(8,128)(2,1)} %constant.10.clone.rf_hbm, bf16[256,544]{1,0:T(8,128)(2,1)} %constant.11.clone.rb_hbm, ...), custom_call_target="tpu_custom_call" | custom-call | tf_op jit(solution)/shard_map/pallas_call | solution.py:258
  48.3 0.7 %copy.11 = bf16[1,256,768]{2,1,0:T(8,128)(2,1)} copy(bf16[1,256,768]{2,1,0:T(8,128)(2,1)S(1)} %bitcast.3) | data formatting | bytes 786432

commit v4 on v3

--- a/solution.py
+++ b/solution.py
@@ -11,6 +11,7 @@
 
 MESH = pl.DeviceIdType.MESH
 COLS = 128
+AHEAD = 12
 
 
 def tables(rows, cols):
@@ -69,6 +70,7 @@
     ys = [lax.rem(q // 8 + d, 4) * 8 for d in range(4)]
     zs = [lax.rem(q + d, 8) for d in range(8)]
     others = far_first((4, 4, 8))
+    ahead = AHEAD
 
     def seq_at(offset):
         return xs[offset[0]] + ys[offset[1]] + zs[offset[2]]
@@ -111,15 +113,33 @@
     by_channel(x_raw, x_send)
     pl.semaphore_wait(barrier, 2 * seqs - 1)
 
-    in_sem = in_sems.at[s]
     to_ref = both_in.at[:, s, :, q]
-    everyone(lambda seq, core: pltpu.make_async_remote_copy(
-        both_send.at[:, pl.ds((seq * 2 + core) * channels, channels)], to_ref,
-        send_sem.at[0], in_sem, device_id={"segment": core, "seq": seq}, device_id_type=MESH,
-    ).start())
-    pltpu.make_async_copy(
-        both_send.at[:, pl.ds(mine * channels, channels)], to_ref, in_sem
-    ).start()
+
+    def send_in(offsets, sem):
+        def go(seq, core):
+            pltpu.make_async_remote_copy(
+                both_send.at[:, pl.ds((seq * 2 + core) * channels, channels)], to_ref,
+                send_sem.at[0], sem, device_id={"segment": core, "seq": seq}, device_id_type=MESH,
+            ).start()
+
+        for offset in offsets:
+            seq = seq_at(offset)
+            go(seq, 1 - s)
+            if any(offset):
+                go(seq, s)
+            else:
+                pltpu.make_async_copy(
+                    both_send.at[:, pl.ds(mine * channels, channels)], to_ref, sem
+                ).start()
+
+    def wait_in(section, count, sem):
+        part = both_in.at[:, section, :, pl.ds(0, count)]
+        pltpu.make_async_copy(part, part, sem).wait()
+
+    @pl.when(s == 0)
+    def _():
+        send_in(others[:ahead], in_sems.at[0])
+        send_in(others[ahead:], in_sems.at[1])
 
     def send_out(section):
         to_ref = y_in.at[pl.ds(mine * channels, channels)]
@@ -195,10 +215,15 @@
                 [jnp.where(b_out >= b_in, circ, 0.0), jnp.where(b_out < b_in, circ, 0.0)], 0
             ).astype(jnp.bfloat16)
 
+    wait_in(0, ahead, in_sems.at[0])
+
+    @pl.when(s == 1)
+    def _():
+        send_in(others, in_sems.at[2])
+
     previous = None
     for section in range(2):
-        part = both_in.at[:, section]
-        pltpu.make_async_copy(part, part, in_sems.at[section]).wait()
+        wait_in(section, seqs if section else seqs - ahead, in_sems.at[1 + section])
         got = spectrum([f_in[section, c].reshape(rows, cols) for c in range(channels)])
         for c in range(channels):
             spec[section, c] = got[c]
@@ -264,7 +289,7 @@
             like(x), like(f), like(short_filters), like(skip_gain), *[like(t) for t in tabs],
             vmem(2, *chunks), vmem(2, *grid), vmem(*grid), vmem(*chunks),
             pltpu.VMEM((2, mine, kept, 2 * cols), jnp.float32), vmem(2, mine, 2 * cols, cols),
-            dma((9,)), dma((2,)), dma((2,)), dma,
+            dma((9,)), dma((2,)), dma((3,)), dma,
         ],
         compiler_params=pltpu.CompilerParams(
             vmem_limit_bytes=54900 * 1024, has_side_effects=True, collective_id=0

time: 49.1 us -> 46 us (0.937)
  Pallas kernels: 48.3 us -> 45.2 us
    pallas_call x1, Pallas kernels: 48.3 us -> 45.2 us  [body(): pl.pallas_call(functools.partial(kernel, scale, kept), out_shape=pltpu.VM...]
where the time goes in v4:
time: 46 us; the launch traced here: 45.9 us
  Pallas kernels  45.2 us (98%)
  local copies, waits for them, and re-layouts  0.75 us (2%)
    pallas_call x1, Pallas kernels, body(): pl.pallas_call(functools.partial(kernel, scale, kept), out_shape=pltpu.VM...  45.2 us

profile of v4, /device:TPU:1, one launch (start us, length us, event | category | flops | bytes accessed | tf_op | source)
XLA Modules:
  0.0 45.9 jit_solution(13278327959467515638)
XLA Ops:
  0.0 45.2 %shard_map.91 = bf16[256,768]{1,0:T(8,128)(2,1)S(1)} custom-call(bf16[256,768]{1,0:T(8,128)(2,1)} %bitcast.5, f32[256,768]{1,0:T(8,128)} %bitcast.4, bf16[2,128,768]{2,1,0:T(8,128)(2,1)} %taps_hbm.1, f32[2,768]{1,0:T(2,128)} %gain_hbm.1, bf16[544,256]{1,0:T(8,128)(2,1)} %constant.10.clone.rf_hbm, bf16[256,544]{1,0:T(8,128)(2,1)} %constant.11.clone.rb_hbm, ...), custom_call_target="tpu_custom_call" | custom-call | tf_op jit(solution)/shard_map/pallas_call | solution.py:283
  45.2 0.7 %copy.11 = bf16[1,256,768]{2,1,0:T(8,128)(2,1)} copy(bf16[1,256,768]{2,1,0:T(8,128)(2,1)S(1)} %bitcast.3) | data formatting | bytes 786432

commit v5 on v4

--- a/solution.py
+++ b/solution.py
@@ -44,7 +44,7 @@
 def far_first(sizes):
     offsets = [(x, y, z) for x in range(sizes[0]) for y in range(sizes[1]) for z in range(sizes[2])]
     hops = lambda o: sum(min(d, n - d) for d, n in zip(o, sizes))
-    return sorted(offsets, key=lambda o: (-hops(o), o))
+    return sorted(offsets, key=lambda o: (-hops(o), o[::-1]))
 
 
 def nt(a, b):

time: 46 us -> 45.5 us (0.989)
  Pallas kernels: 45.2 us -> 44.7 us
    pallas_call x1, Pallas kernels: 45.2 us -> 44.7 us  [body(): pl.pallas_call(functools.partial(kernel, scale, kept), out_shape=pltpu.VM...]
where the time goes in v5:
time: 45.5 us
  Pallas kernels  44.7 us (98%)
  local copies, waits for them, and re-layouts  0.75 us (2%)
    pallas_call x1, Pallas kernels, body(): pl.pallas_call(functools.partial(kernel, scale, kept), out_shape=pltpu.VM...  44.7 us

profile of v5, /device:TPU:1, one launch (start us, length us, event | category | flops | bytes accessed | tf_op | source)
XLA Modules:
  0.0 45.5 jit_solution(12218581280663035046)
XLA Ops:
  0.0 44.7 %shard_map.91 = bf16[256,768]{1,0:T(8,128)(2,1)S(1)} custom-call(bf16[256,768]{1,0:T(8,128)(2,1)} %bitcast.5, f32[256,768]{1,0:T(8,128)} %bitcast.4, bf16[2,128,768]{2,1,0:T(8,128)(2,1)} %taps_hbm.1, f32[2,768]{1,0:T(2,128)} %gain_hbm.1, bf16[544,256]{1,0:T(8,128)(2,1)} %constant.10.clone.rf_hbm, bf16[256,544]{1,0:T(8,128)(2,1)} %constant.11.clone.rb_hbm, ...), custom_call_target="tpu_custom_call" | custom-call | tf_op jit(solution)/shard_map/pallas_call | solution.py:283
  44.7 0.7 %copy.11 = bf16[1,256,768]{2,1,0:T(8,128)(2,1)} copy(bf16[1,256,768]{2,1,0:T(8,128)(2,1)S(1)} %bitcast.3) | data formatting | bytes 786432
